TPU v7x, 512 devices: a whole 4x8x8 slice. The times are simulated.
512 devices in a mesh: slab: 128 (over z, x, y_lo), sec: 4 (over y_hi, core).
Axes of the slice: x: 4, y: 8 (y_hi: 2, y_lo: 4; y = y_hi * 4 + y_lo), z: 8, core: 2. Of those that a mesh axis runs over, the one named last changes fastest.
Arguments:
- displacement: float32 [5120, 4096], P('slab', 'sec'), may hold values from -6 to 6
- earlier_field: float32 [5120, 4096], P('slab', 'sec'), may hold values from -6 to 6
- region_ids: int32 [4096], P('sec'), may hold values from 0 to 7
- material: float32 [2, 8], replicated, may hold values from 0.5 to 1.5
- mode_shapes: float32 [4096, 64], P('sec'), may hold values from -0.75 to 0.75
- band_edges: int32 [2, 64], replicated, may hold values from 0 to 4095, as said below
Outputs:
- advanced_field: float32 [5120, 4096], P('slab', 'sec')
- band_field: bfloat16 [5120, 4096], P('slab', 'sec')
Inputs may be any that keep to these rules, and one draw needn't show every extreme that they name: `band_edges`: for every mode the lower edge is below the upper edge; some mode's band starts at 0 and some mode's band ends at 4095.
All inputs are finite; a program needn't handle non-finite values.
Results may differ from a plain program's by a relative error of at most 0.001.
Values sent between devices are 32-bit elements; how exact they have to be, the bound alone decides.
A program may use at most 64 MiB of HBM per device.

v0:
```python
import math
import jax
import jax.numpy as jnp
from jax import lax
from jax.sharding import PartitionSpec as P

COLS = 64
MODES = 64
WAVES = 4096
REGIONS = 8
STEPS = 4
courant_sq = 0.14
two_pi = 2.0 * math.pi


def extended_2(x, sides, width, wrap):
    for axis, dim in sides:
        peers, length = (lax.axis_size(axis), x.shape[dim])
        up = [(i, (i + 1) % peers) for i in range(peers if wrap else peers - 1)]
        down = [(j, i) for i, j in up]
        last = lax.slice_in_dim(x, length - width, length, axis=dim)
        leading = lax.slice_in_dim(x, 0, width, axis=dim)
        before = lax.ppermute(last, axis, up)
        after = lax.ppermute(leading, axis, down)
        x = jnp.concatenate([before, x, after], axis=dim)
    return x


def lookup_stiffness(region_ids, material):
    values = courant_sq * material[0] * material[1]
    match = region_ids[:, None] == jnp.arange(REGIONS, dtype=jnp.int32)[None, :]
    return jnp.sum(jnp.where(match, values[None, :], jnp.zeros_like(values)[None, :]), axis=1)


def advance(extended, before, stiffness):
    centre = extended[1:-1]
    cells_here = centre.shape[1]
    widened = extended_2(centre, (("sec", 1),), COLS, False)
    above = widened[:, :cells_here]
    below = widened[:, 2 * COLS :]
    planar = centre.reshape(centre.shape[0], cells_here // COLS, COLS)
    west_cells = jnp.pad(planar[:, :, :-1], ((0, 0), (0, 0), (1, 0))).reshape(centre.shape)
    east_cells = jnp.pad(planar[:, :, 1:], ((0, 0), (0, 0), (0, 1))).reshape(centre.shape)
    summed = extended[2:] + extended[:-2] + above + below + west_cells + east_cells
    return 2.0 * centre - before + stiffness[None, :] * (summed - 6.0 * centre)


def phases(first, second, period_len):
    product = first[:, None] * second[None, :]
    return (product % period_len).astype(jnp.float32) * (two_pi / period_len)


def body(displacement, earlier_field, region_ids, material, mode_shapes, band_edges):
    planes_here = displacement.shape[0]
    period_len = planes_here * lax.axis_size("slab")
    stiffness = lookup_stiffness(region_ids, material)
    current, before = (displacement, earlier_field)
    for _ in range(STEPS):
        extended = extended_2(current, (("slab", 0),), 1, True)
        current, before = (advance(extended, before, stiffness), current)
    modal_part = jnp.dot(current, mode_shapes, precision=lax.Precision.HIGHEST)
    plane_ids = lax.axis_index("slab") * planes_here + jnp.arange(planes_here, dtype=jnp.int32)
    lower_edge = jnp.concatenate([band_edges[0], band_edges[0]])[None, :]
    upper_edge = jnp.concatenate([band_edges[1], band_edges[1]])[None, :]
    empty = jnp.zeros((planes_here, MODES), jnp.float32)
    modal = lax.psum(modal_part, "sec")
    owned_rows = WAVES // lax.axis_size("slab")
    row_count = owned_rows * lax.axis_size("slab")
    block_len = min(row_count, 512)

    def make_one_block(index):
        wavenums = index * block_len + jnp.arange(block_len, dtype=jnp.int32)
        angle = phases(wavenums, plane_ids, period_len)
        return jnp.concatenate(
            [
                jnp.dot(jnp.cos(angle), modal, precision=lax.Precision.HIGHEST),
                jnp.dot(jnp.sin(angle), modal, precision=lax.Precision.HIGHEST),
            ],
            axis=1,
        )

    result = lax.map(make_one_block, jnp.arange(row_count // block_len, dtype=jnp.int32))
    owned = lax.psum_scatter(
        result.reshape(row_count, 2 * MODES), "slab", scatter_dimension=0, tiled=True
    )
    wavenums = (
        lax.axis_index("slab") * owned_rows + jnp.arange(owned.shape[0], dtype=jnp.int32)[:, None]
    )
    in_band = (wavenums >= lower_edge) & (wavenums < upper_edge)
    filtered = jnp.where(in_band, owned, jnp.zeros_like(owned))
    running = empty
    portion = lax.all_gather(filtered, "slab", axis=0, tiled=True)
    row_count = portion.shape[0]
    inverse_block_len = min(row_count, 512)
    portions = portion.reshape(row_count // inverse_block_len, inverse_block_len, 2 * MODES)

    def inverse_one_block(inner, item):
        index, piece_rows = item
        wavenums = index * inverse_block_len + jnp.arange(inverse_block_len, dtype=jnp.int32)
        angle = phases(plane_ids, wavenums, period_len)
        inner = inner + jnp.dot(
            jnp.cos(angle), piece_rows[:, :MODES], precision=lax.Precision.HIGHEST
        )
        inner = inner + jnp.dot(
            jnp.sin(angle), piece_rows[:, MODES:], precision=lax.Precision.HIGHEST
        )
        return (inner, None)

    running, _ = lax.scan(
        inverse_one_block,
        running,
        (jnp.arange(row_count // inverse_block_len, dtype=jnp.int32), portions),
    )
    smooth = running
    smooth = smooth * (2.0 / period_len)
    band_field = jnp.dot(smooth, mode_shapes.T, precision=lax.Precision.HIGHEST).astype(
        jnp.bfloat16
    )
    return (current, band_field)


def solution(mesh):
    return jax.shard_map(
        body,
        mesh=mesh,
        in_specs=(P("slab", "sec"), P("slab", "sec"), P("sec"), P(), P("sec", None), P()),
        out_specs=(P("slab", "sec"), P("slab", "sec")),
        check_vma=False,
    )
```

profile of v0, /device:TPU:32, one launch (start us, length us, event | category | flops | bytes accessed | tf_op | source)
XLA Modules:
  0.0 1638.3 jit_solution(503849871708262057)
XLA Ops:
  8.1 1.9 collective-permute-start.2
  10.1 7.5 collective-permute-start.3
  18.4 13.5 collective-permute-start
  31.9 1.9 collective-permute-start.1
  37.0 6.4 collective-permute-done.1
  43.8 1.9 collective-permute-start.6
  45.7 7.5 collective-permute-start.7
  53.3 3.6 collective-permute-start.4
  56.9 2.2 collective-permute-start.5
  59.8 8.8 collective-permute-done.5
  68.9 1.9 collective-permute-start.10
  70.9 7.5 collective-permute-start.11
  78.4 1.9 collective-permute-start.8
  80.4 3.9 collective-permute-start.9
  84.9 6.9 collective-permute-done.9
  92.3 1.9 collective-permute-start.14
  94.2 7.5 collective-permute-start.15
  101.7 1.9 collective-permute-start.12
  103.7 3.9 collective-permute-start.13
  108.2 6.9 collective-permute-done.13
  115.7 18.1 %psum.7 = f32[40,64]{1,0:T(8,128)S(1)} all-reduce(f32[40,64]{1,0:T(8,128)S(1)} %fusion.105), channel_id=1, replica_groups=mesh['slab'=128,'sec'=4] {'sec'}, use_global_device_ids=true, to_apply=%region_1.2 | all-reduce | flops 2560 | bytes 20480 | tf_op jit(solution)/shard_map/psum | solution.py:66
  133.8 41.0 %while.26 = (s32[]{:T(128)}, f32[8,512,128]{2,1,0:T(8,128)}, s32[8]{0:T(128)S(1)}, f32[40,64]{1,0:T(8,128)S(1)}, s32[]{:T(128)}, /*index=5*/s32[]{:T(128)}, s32[1]{0:T(128)}) while((s32[]{:T(128)}, f32[8,512,128]{2,1,0:T(8,128)}, s32[8]{0:T(128)S(1)}, f32[40,64]{1,0:T(8,128)S(1)}, s32[]{:T(128)}, /*index=5*/s32[]{:T(128)}, ...), condition=%wide.region_3.4_spmd.clone, body=%wide.region_2.3_spmd.clone.sunk | while | flops 31892012 | bytes 1862733 | solution.py:82
  135.2 1.5 fusion.125
  140.3 1.5 fusion.125
  145.4 1.5 fusion.125
  155.7 1.5 fusion.125
  160.8 1.5 fusion.125
  165.9 1.5 fusion.125
  171.1 1.5 fusion.125
  175.6 738.4 %reduce-scatter.2.cloned.1.call-done = f32[32,128]{1,0:T(8,128)} async-done(((f32[4096,128]{1,0:T(8,128)}), f32[32,128]{1,0:T(8,128)}) %reduce-scatter.2.cloned.1.call-update) | async-done | bytes 16400 | tf_op jit(solution)/shard_map/reduce_scatter | solution.py:83
  915.5 686.4 %all-gather.2.cloned.1.call-done = f32[4096,128]{1,0:T(8,128)} async-done(((f32[32,128]{1,0:T(8,128)}), f32[4096,128]{1,0:T(8,128)}) %all-gather.2.cloned.1.call-update) | async-done | bytes 2097168 | tf_op jit(solution)/shard_map/all_gather | solution.py:92
  1601.9 28.6 %while.27 = (s32[]{:T(128)}, f32[40,64]{1,0:T(8,128)S(1)}, s32[8]{0:T(128)S(1)}, f32[8,512,128]{2,1,0:T(8,128)}, s32[]{:T(128)}, /*index=5*/s32[]{:T(128)}, s32[1]{0:T(128)}, s32[]{:T(128)}) while((s32[]{:T(128)}, f32[40,64]{1,0:T(8,128)S(1)}, s32[8]{0:T(128)S(1)}, f32[8,512,128]{2,1,0:T(8,128)}, s32[]{:T(128)}, ...), condition=%wide.region_6.7_spmd.clone, body=%wide.region_5.6_spmd.clone.sunk | while | flops 31834156 | bytes 1096291 | solution.py:109
  (179 shorter events, 59.6 us)
Async XLA Ops:
  7.2 108.2 %copy-start = (f32[1024,64]{0,1:T(8,128)S(1)}, f32[1024,64]{0,1:T(8,128)}, u32[]{:S(2)}) copy-start(f32[1024,64]{0,1:T(8,128)} %param.14) | copy-start | bytes 786436
  7.2 36.2 %copy-start.1 = (f32[40,1024]{1,0:T(8,128)S(1)}, f32[40,1024]{1,0:T(8,128)}, u32[]{:S(2)}) copy-start(f32[40,1024]{1,0:T(8,128)} %param.10) | copy-start | bytes 491524
  7.2 36.2 %copy-start.3 = (f32[40,1024]{1,0:T(8,128)S(1)}, f32[40,1024]{1,0:T(8,128)}, u32[]{:S(2)}) copy-start(f32[40,1024]{1,0:T(8,128)} %param.11) | copy-start | bytes 491524
  7.2 906.9 %reduce-scatter.2.cloned.1.call-start = ((), (), s32[]{:S(2)}) async-start(), calls=%async_computation.1 | async-start | bytes 2113536 | tf_op jit(solution)/shard_map/reduce_scatter | solution.py:83
  8.1 35.3 %collective-permute-start.2 = (f32[40,64]{1,0:T(8,128)S(1)}, f32[40,64]{1,0:T(8,128)S(1)}, u32[]{:S(2)}, u32[]{:S(2)}) collective-permute-start(f32[40,64]{1,0:T(8,128)S(1)} %get-tuple-element.212), channel_id=1, source_target_pairs={{0,1},{1,2},{2,3},{4,5},{5,6},{6,7},{8,9},{9,10},{10,11},{12,13},{... | collective-permute-start | bytes 30728 | tf_op jit(solution)/shard_map/ppermute | solution.py:23
  10.1 33.3 %collective-permute-start.3 = (f32[40,64]{1,0:T(8,128)S(1)}, f32[40,64]{1,0:T(8,128)S(1)}, u32[]{:S(2)}, u32[]{:S(2)}) collective-permute-start(f32[40,64]{1,0:T(8,128)S(1)} %get-tuple-element.213), channel_id=1, source_target_pairs={{1,0},{2,1},{3,2},{5,4},{6,5},{7,6},{9,8},{10,9},{11,10},{13,12},{... | collective-permute-start | bytes 30728 | tf_op jit(solution)/shard_map/ppermute | solution.py:24
  18.4 18.6 %collective-permute-start = (f32[1,1024]{1,0:T(1,128)S(1)}, f32[1,1024]{1,0:T(1,128)S(1)}, u32[]{:S(2)}, u32[]{:S(2)}) collective-permute-start(f32[1,1024]{1,0:T(1,128)S(1)} %get-tuple-element.210), channel_id=1, source_target_pairs={{4,0},{8,4},{12,8},{16,12},{20,16},{24,20},{28,24},{32,28},{36,32}... | collective-permute-start | bytes 12296 | tf_op jit(solution)/shard_map/ppermute | solution.py:24
  31.9 11.5 collective-permute-start.1
  43.8 24.8 %collective-permute-start.6 = (f32[40,64]{1,0:T(8,128)S(1)}, f32[40,64]{1,0:T(8,128)S(1)}, u32[]{:S(2)}, u32[]{:S(2)}) collective-permute-start(f32[40,64]{1,0:T(8,128)S(1)} %get-tuple-element.208), channel_id=1, source_target_pairs={{0,1},{1,2},{2,3},{4,5},{5,6},{6,7},{8,9},{9,10},{10,11},{12,13},{... | collective-permute-start | bytes 30728 | tf_op jit(solution)/shard_map/ppermute | solution.py:23
  45.7 22.8 %collective-permute-start.7 = (f32[40,64]{1,0:T(8,128)S(1)}, f32[40,64]{1,0:T(8,128)S(1)}, u32[]{:S(2)}, u32[]{:S(2)}) collective-permute-start(f32[40,64]{1,0:T(8,128)S(1)} %get-tuple-element.209), channel_id=1, source_target_pairs={{1,0},{2,1},{3,2},{5,4},{6,5},{7,6},{9,8},{10,9},{11,10},{13,12},{... | collective-permute-start | bytes 30728 | tf_op jit(solution)/shard_map/ppermute | solution.py:24
  53.3 6.5 collective-permute-start.4
  56.9 11.7 collective-permute-start.5
  68.9 22.9 %collective-permute-start.10 = (f32[40,64]{1,0:T(8,128)S(1)}, f32[40,64]{1,0:T(8,128)S(1)}, u32[]{:S(2)}, u32[]{:S(2)}) collective-permute-start(f32[40,64]{1,0:T(8,128)S(1)} %get-tuple-element.204), channel_id=1, source_target_pairs={{0,1},{1,2},{2,3},{4,5},{5,6},{6,7},{8,9},{9,10},{10,11},{12,13},{... | collective-permute-start | bytes 30728 | tf_op jit(solution)/shard_map/ppermute | solution.py:23
  70.9 21.0 %collective-permute-start.11 = (f32[40,64]{1,0:T(8,128)S(1)}, f32[40,64]{1,0:T(8,128)S(1)}, u32[]{:S(2)}, u32[]{:S(2)}) collective-permute-start(f32[40,64]{1,0:T(8,128)S(1)} %get-tuple-element.205), channel_id=1, source_target_pairs={{1,0},{2,1},{3,2},{5,4},{6,5},{7,6},{9,8},{10,9},{11,10},{13,12},{... | collective-permute-start | bytes 30728 | tf_op jit(solution)/shard_map/ppermute | solution.py:24
  78.4 6.5 collective-permute-start.8
  80.4 11.5 collective-permute-start.9
  92.3 22.9 %collective-permute-start.14 = (f32[40,64]{1,0:T(8,128)S(1)}, f32[40,64]{1,0:T(8,128)S(1)}, u32[]{:S(2)}, u32[]{:S(2)}) collective-permute-start(f32[40,64]{1,0:T(8,128)S(1)} %get-tuple-element.200), channel_id=1, source_target_pairs={{0,1},{1,2},{2,3},{4,5},{5,6},{6,7},{8,9},{9,10},{10,11},{12,13},{... | collective-permute-start | bytes 30728 | tf_op jit(solution)/shard_map/ppermute | solution.py:23
  94.2 21.0 %collective-permute-start.15 = (f32[40,64]{1,0:T(8,128)S(1)}, f32[40,64]{1,0:T(8,128)S(1)}, u32[]{:S(2)}, u32[]{:S(2)}) collective-permute-start(f32[40,64]{1,0:T(8,128)S(1)} %get-tuple-element.201), channel_id=1, source_target_pairs={{1,0},{2,1},{3,2},{5,4},{6,5},{7,6},{9,8},{10,9},{11,10},{13,12},{... | collective-permute-start | bytes 30728 | tf_op jit(solution)/shard_map/ppermute | solution.py:24
  101.7 6.5 collective-permute-start.12
  103.7 11.5 collective-permute-start.13
  115.4 18.4 %copy-start.2 = (f32[40,1024]{1,0:T(8,128)}, f32[40,1024]{1,0:T(8,128)S(1)}, u32[]{:S(2)}) copy-start(f32[40,1024]{1,0:T(8,128)S(1)} %fusion.63) | copy-start | bytes 491524
  174.9 0.7 copy-start.4
  174.9 1427.0 %all-gather.2.cloned.1.call-start = ((), (), s32[]{:S(2)}) async-start(), calls=%async_computation.2 | async-start | bytes 2113536 | tf_op jit(solution)/shard_map/all_gather | solution.py:92
Sparse Core Ops, SparseCore 0:
  175.0 738.9 reduce-scatter.1
  916.7 685.1 all-gather.1
where the time goes:
time: 1640 us
  waiting for transfers between devices  1450 us (88%)
  starting transfers between devices  70.9 us (4%)
  matrix products  34.8 us (2%)
  local copies, waits for them, and re-layouts  30.8 us (2%)
  blocking collectives  18.1 us (1%)
    reduce_scatter x1, waiting for transfers between devices, body(): lax.psum_scatter(result.reshape(row_count, 2 * MODES), 'slab', scatter_di...  738 us
    all_gather x1, waiting for transfers between devices, body(): portion = lax.all_gather(filtered, 'slab', axis=0, tiled=True)  686 us
    ppermute x8, starting transfers between devices, extended_2(): after = lax.ppermute(leading, axis, down)  51.1 us
  transfers between devices with their start and end apart: 18, of which 6 were waited for; matrix products, arithmetic and copies ran while one was open for 0% of the time, Pallas kernels for 0%

commit v1 on v0

--- a/solution.py
+++ b/solution.py
@@ -89,7 +89,9 @@
     in_band = (wavenums >= lower_edge) & (wavenums < upper_edge)
     filtered = jnp.where(in_band, owned, jnp.zeros_like(owned))
     running = empty
-    portion = lax.all_gather(filtered, "slab", axis=0, tiled=True)
+    portion = jnp.concatenate(
+        lax.all_to_all(jnp.stack([filtered] * lax.axis_size("slab")), "slab", 0, 0), axis=0
+    )
     row_count = portion.shape[0]
     inverse_block_len = min(row_count, 512)
     portions = portion.reshape(row_count // inverse_block_len, inverse_block_len, 2 * MODES)

time: 1640 us -> 989 us (0.60)
  the two profiles are of different devices: /device:TPU:32 before, /device:TPU:56 now
where the time goes in v1:
time: 989 us; the launch traced here: 988 us
  waiting for transfers between devices  782 us (79%)
  starting transfers between devices  99.5 us (10%)
  matrix products  34.8 us (4%)
  local copies, waits for them, and re-layouts  24.9 us (3%)
  blocking collectives  18.1 us (2%)
  between operations  14.5 us (1%)
  loops' own time  10.4 us (1%)
    reduce_scatter x1, waiting for transfers between devices, body(): lax.psum_scatter(result.reshape(row_count, 2 * MODES), 'slab', scatter_di...  740 us
    ppermute x8, starting transfers between devices, extended_2(): after = lax.ppermute(leading, axis, down)  55.1 us
    all_to_all x1, waiting for transfers between devices, body(): lax.all_to_all(jnp.stack([filtered] * lax.axis_size('slab')), 'slab', 0, 0)  30.9 us
    ppermute x8, starting transfers between devices, extended_2(): before = lax.ppermute(last, axis, up)  23.4 us
    all_to_all x1, starting transfers between devices, body(): lax.all_to_all(jnp.stack([filtered] * lax.axis_size('slab')), 'slab', 0, 0)  21 us
  transfers between devices with their start and end apart: 18, of which 5 were waited for; matrix products, arithmetic and copies ran while one was open for 1% of the time, Pallas kernels for 0%

profile of v1, /device:TPU:56, one launch (start us, length us, event | category | flops | bytes accessed | tf_op | source)
XLA Modules:
  0.0 987.9 jit_solution(2345344725090687751)
XLA Ops:
  8.1 1.9 collective-permute-start.2
  10.1 7.5 collective-permute-start.3
  18.4 3.2 collective-permute-start
  21.7 5.3 collective-permute-start.1
  30.6 1.9 collective-permute-start.6
  32.5 7.5 collective-permute-start.7
  40.1 1.9 collective-permute-start.4
  42.0 6.6 collective-permute-start.5
  49.3 5.4 collective-permute-done.5
  55.1 1.9 collective-permute-start.10
  57.0 7.5 collective-permute-start.11
  64.6 9.9 %collective-permute-start.8 = (f32[1,1024]{1,0:T(1,128)S(1)}, f32[1,1024]{1,0:T(1,128)S(1)}, u32[]{:S(2)}, u32[]{:S(2)}) collective-permute-start(f32[1,1024]{1,0:T(1,128)S(1)} %get-tuple-element.202), channel_id=1, source_target_pairs={{4,0},{8,4},{12,8},{16,12},{20,16},{24,20},{28,24},{32,28},{36,32}... | collective-permute-start | bytes 12296 | tf_op jit(solution)/shard_map/ppermute | solution.py:24
  74.5 1.9 collective-permute-start.9
  77.1 2.9 collective-permute-done.9
  80.4 1.9 collective-permute-start.14
  82.3 7.5 collective-permute-start.15
  89.9 9.8 collective-permute-start.12
  99.7 1.9 collective-permute-start.13
  102.2 2.9 collective-permute-done.13
  105.7 18.1 %psum.7 = f32[40,64]{1,0:T(8,128)S(1)} all-reduce(f32[40,64]{1,0:T(8,128)S(1)} %fusion.105), channel_id=1, replica_groups=mesh['slab'=128,'sec'=4] {'sec'}, use_global_device_ids=true, to_apply=%region_1.2 | all-reduce | flops 2560 | bytes 20480 | tf_op jit(solution)/shard_map/psum | solution.py:66
  123.8 39.7 %while.26 = (s32[]{:T(128)}, f32[8,512,128]{2,1,0:T(8,128)}, s32[8]{0:T(128)S(1)}, f32[40,64]{1,0:T(8,128)S(1)}, s32[]{:T(128)}, /*index=5*/s32[]{:T(128)}, s32[1]{0:T(128)}) while((s32[]{:T(128)}, f32[8,512,128]{2,1,0:T(8,128)}, s32[8]{0:T(128)S(1)}, f32[40,64]{1,0:T(8,128)S(1)}, s32[]{:T(128)}, /*index=5*/s32[]{:T(128)}, ...), condition=%wide.region_3.4_spmd.clone, body=%wide.region_2.3_spmd.clone.sunk | while | flops 31892012 | bytes 1862733 | solution.py:82
  125.0 1.5 fusion.125
  129.9 1.5 fusion.125
  134.9 1.5 fusion.125
  139.8 1.5 fusion.125
  154.7 1.5 fusion.125
  159.7 1.5 fusion.125
  164.2 740.0 %reduce-scatter.2.cloned.1.call-done = f32[32,128]{1,0:T(8,128)} async-done(((f32[4096,128]{1,0:T(8,128)}), f32[32,128]{1,0:T(8,128)}) %reduce-scatter.2.cloned.1.call-update) | async-done | bytes 16400 | tf_op jit(solution)/shard_map/reduce_scatter | solution.py:83
  905.1 1.6 stack.2
  906.7 21.0 %all-to-all-start = ((f32[128,32,128]{2,1,0:T(8,128)}), f32[128,32,128]{2,1,0:T(8,128)S(1)}, u32[]{:S(2)}, u32[]{:S(2)}) async-start(f32[128,32,128]{2,1,0:T(8,128)} %stack.2), calls=%async_computation.1 | async-start | bytes 4194304 | tf_op jit(solution)/shard_map/all_to_all | solution.py:93
  927.7 30.9 %all-to-all-done = f32[128,32,128]{2,1,0:T(8,128)S(1)} async-done(((f32[128,32,128]{2,1,0:T(8,128)}), f32[128,32,128]{2,1,0:T(8,128)S(1)}, u32[]{:S(2)}, u32[]{:S(2)}) %all-to-all-start) | async-done | bytes 2097184 | tf_op jit(solution)/shard_map/all_to_all | solution.py:93
  958.5 21.5 %while.27 = (s32[]{:T(128)}, f32[40,64]{1,0:T(8,128)S(1)}, s32[8]{0:T(128)S(1)}, f32[8,512,128]{2,1,0:T(8,128)S(1)}, s32[]{:T(128)}, /*index=5*/s32[]{:T(128)}, s32[1]{0:T(128)}, s32[]{:T(128)}) while((s32[]{:T(128)}, f32[40,64]{1,0:T(8,128)S(1)}, s32[8]{0:T(128)S(1)}, f32[8,512,128]{2,1,0:T(8,128)S(1)}, s32[]{:T(128)}, ...), condition=%wide.region_6.7_spmd.clone, body=%wide.region_5.6_spmd.clone.sunk | while | flops 31834156 | bytes 1096291 | solution.py:111
  (179 shorter events, 52.9 us)
Async XLA Ops:
  7.2 98.2 %copy-start = (f32[1024,64]{0,1:T(8,128)S(1)}, f32[1024,64]{0,1:T(8,128)}, u32[]{:S(2)}) copy-start(f32[1024,64]{0,1:T(8,128)} %param.14) | copy-start | bytes 786436
  7.2 23.0 %copy-start.1 = (f32[40,1024]{1,0:T(8,128)S(1)}, f32[40,1024]{1,0:T(8,128)}, u32[]{:S(2)}) copy-start(f32[40,1024]{1,0:T(8,128)} %param.10) | copy-start | bytes 491524
  7.2 23.0 %copy-start.3 = (f32[40,1024]{1,0:T(8,128)S(1)}, f32[40,1024]{1,0:T(8,128)}, u32[]{:S(2)}) copy-start(f32[40,1024]{1,0:T(8,128)} %param.11) | copy-start | bytes 491524
  7.2 897.1 %reduce-scatter.2.cloned.1.call-start = ((), (), s32[]{:S(2)}) async-start(), calls=%async_computation.2 | async-start | bytes 2113536 | tf_op jit(solution)/shard_map/reduce_scatter | solution.py:83
  8.1 22.0 %collective-permute-start.2 = (f32[40,64]{1,0:T(8,128)S(1)}, f32[40,64]{1,0:T(8,128)S(1)}, u32[]{:S(2)}, u32[]{:S(2)}) collective-permute-start(f32[40,64]{1,0:T(8,128)S(1)} %get-tuple-element.212), channel_id=1, source_target_pairs={{0,1},{1,2},{2,3},{4,5},{5,6},{6,7},{8,9},{9,10},{10,11},{12,13},{... | collective-permute-start | bytes 30728 | tf_op jit(solution)/shard_map/ppermute | solution.py:23
  10.1 20.1 %collective-permute-start.3 = (f32[40,64]{1,0:T(8,128)S(1)}, f32[40,64]{1,0:T(8,128)S(1)}, u32[]{:S(2)}, u32[]{:S(2)}) collective-permute-start(f32[40,64]{1,0:T(8,128)S(1)} %get-tuple-element.213), channel_id=1, source_target_pairs={{1,0},{2,1},{3,2},{5,4},{6,5},{7,6},{9,8},{10,9},{11,10},{13,12},{... | collective-permute-start | bytes 30728 | tf_op jit(solution)/shard_map/ppermute | solution.py:24
  18.4 11.8 %collective-permute-start = (f32[1,1024]{1,0:T(1,128)S(1)}, f32[1,1024]{1,0:T(1,128)S(1)}, u32[]{:S(2)}, u32[]{:S(2)}) collective-permute-start(f32[1,1024]{1,0:T(1,128)S(1)} %get-tuple-element.210), channel_id=1, source_target_pairs={{4,0},{8,4},{12,8},{16,12},{20,16},{24,20},{28,24},{32,28},{36,32}... | collective-permute-start | bytes 12296 | tf_op jit(solution)/shard_map/ppermute | solution.py:24
  21.7 8.5 collective-permute-start.1
  30.6 24.1 %collective-permute-start.6 = (f32[40,64]{1,0:T(8,128)S(1)}, f32[40,64]{1,0:T(8,128)S(1)}, u32[]{:S(2)}, u32[]{:S(2)}) collective-permute-start(f32[40,64]{1,0:T(8,128)S(1)} %get-tuple-element.208), channel_id=1, source_target_pairs={{0,1},{1,2},{2,3},{4,5},{5,6},{6,7},{8,9},{9,10},{10,11},{12,13},{... | collective-permute-start | bytes 30728 | tf_op jit(solution)/shard_map/ppermute | solution.py:23
  32.5 22.2 %collective-permute-start.7 = (f32[40,64]{1,0:T(8,128)S(1)}, f32[40,64]{1,0:T(8,128)S(1)}, u32[]{:S(2)}, u32[]{:S(2)}) collective-permute-start(f32[40,64]{1,0:T(8,128)S(1)} %get-tuple-element.209), channel_id=1, source_target_pairs={{1,0},{2,1},{3,2},{5,4},{6,5},{7,6},{9,8},{10,9},{11,10},{13,12},{... | collective-permute-start | bytes 30728 | tf_op jit(solution)/shard_map/ppermute | solution.py:24
  40.1 9.2 collective-permute-start.4
  42.0 12.7 %collective-permute-start.5 = (f32[1,1024]{1,0:T(1,128)S(1)}, f32[1,1024]{1,0:T(1,128)S(1)}, u32[]{:S(2)}, u32[]{:S(2)}) collective-permute-start(f32[1,1024]{1,0:T(1,128)S(1)} %get-tuple-element.207), channel_id=1, source_target_pairs={{0,4},{4,8},{8,12},{12,16},{16,20},{20,24},{24,28},{28,32},{32,36}... | collective-permute-start | bytes 12296 | tf_op jit(solution)/shard_map/ppermute | solution.py:23
  55.1 24.9 %collective-permute-start.10 = (f32[40,64]{1,0:T(8,128)S(1)}, f32[40,64]{1,0:T(8,128)S(1)}, u32[]{:S(2)}, u32[]{:S(2)}) collective-permute-start(f32[40,64]{1,0:T(8,128)S(1)} %get-tuple-element.204), channel_id=1, source_target_pairs={{0,1},{1,2},{2,3},{4,5},{5,6},{6,7},{8,9},{9,10},{10,11},{12,13},{... | collective-permute-start | bytes 30728 | tf_op jit(solution)/shard_map/ppermute | solution.py:23
  57.0 23.0 %collective-permute-start.11 = (f32[40,64]{1,0:T(8,128)S(1)}, f32[40,64]{1,0:T(8,128)S(1)}, u32[]{:S(2)}, u32[]{:S(2)}) collective-permute-start(f32[40,64]{1,0:T(8,128)S(1)} %get-tuple-element.205), channel_id=1, source_target_pairs={{1,0},{2,1},{3,2},{5,4},{6,5},{7,6},{9,8},{10,9},{11,10},{13,12},{... | collective-permute-start | bytes 30728 | tf_op jit(solution)/shard_map/ppermute | solution.py:24
  64.6 12.5 %collective-permute-start.8 = (f32[1,1024]{1,0:T(1,128)S(1)}, f32[1,1024]{1,0:T(1,128)S(1)}, u32[]{:S(2)}, u32[]{:S(2)}) collective-permute-start(f32[1,1024]{1,0:T(1,128)S(1)} %get-tuple-element.202), channel_id=1, source_target_pairs={{4,0},{8,4},{12,8},{16,12},{20,16},{24,20},{28,24},{32,28},{36,32}... | collective-permute-start | bytes 12296 | tf_op jit(solution)/shard_map/ppermute | solution.py:24
  74.5 5.5 collective-permute-start.9
  80.4 24.8 %collective-permute-start.14 = (f32[40,64]{1,0:T(8,128)S(1)}, f32[40,64]{1,0:T(8,128)S(1)}, u32[]{:S(2)}, u32[]{:S(2)}) collective-permute-start(f32[40,64]{1,0:T(8,128)S(1)} %get-tuple-element.200), channel_id=1, source_target_pairs={{0,1},{1,2},{2,3},{4,5},{5,6},{6,7},{8,9},{9,10},{10,11},{12,13},{... | collective-permute-start | bytes 30728 | tf_op jit(solution)/shard_map/ppermute | solution.py:23
  82.3 22.8 %collective-permute-start.15 = (f32[40,64]{1,0:T(8,128)S(1)}, f32[40,64]{1,0:T(8,128)S(1)}, u32[]{:S(2)}, u32[]{:S(2)}) collective-permute-start(f32[40,64]{1,0:T(8,128)S(1)} %get-tuple-element.201), channel_id=1, source_target_pairs={{1,0},{2,1},{3,2},{5,4},{6,5},{7,6},{9,8},{10,9},{11,10},{13,12},{... | collective-permute-start | bytes 30728 | tf_op jit(solution)/shard_map/ppermute | solution.py:24
  89.9 12.3 %collective-permute-start.12 = (f32[1,1024]{1,0:T(1,128)S(1)}, f32[1,1024]{1,0:T(1,128)S(1)}, u32[]{:S(2)}, u32[]{:S(2)}) collective-permute-start(f32[1,1024]{1,0:T(1,128)S(1)} %get-tuple-element.198), channel_id=1, source_target_pairs={{4,0},{8,4},{12,8},{16,12},{20,16},{24,20},{28,24},{32,28},{36,32}... | collective-permute-start | bytes 12296 | tf_op jit(solution)/shard_map/ppermute | solution.py:24
  99.7 5.5 collective-permute-start.13
  105.4 18.4 %copy-start.2 = (f32[40,1024]{1,0:T(8,128)}, f32[40,1024]{1,0:T(8,128)S(1)}, u32[]{:S(2)}) copy-start(f32[40,1024]{1,0:T(8,128)S(1)} %fusion.63) | copy-start | bytes 491524
  163.5 0.7 copy-start.4
  906.7 51.9 %all-to-all-start = ((f32[128,32,128]{2,1,0:T(8,128)}), f32[128,32,128]{2,1,0:T(8,128)S(1)}, u32[]{:S(2)}, u32[]{:S(2)}) async-start(f32[128,32,128]{2,1,0:T(8,128)} %stack.2), calls=%async_computation.1 | async-start | bytes 4194304 | tf_op jit(solution)/shard_map/all_to_all | solution.py:93
Sparse Core Ops, SparseCore 0:
  163.6 740.5 reduce-scatter.1
